TPU v7x, 256 devices: a whole 4x4x8 slice. The times are simulated.
256 devices in a mesh: seq: 32 (over x, z_lo, core), chan: 8 (over y, z_hi).
Axes of the slice: x: 4, y: 4, z: 8 (z_hi: 2, z_lo: 4; z = z_hi * 4 + z_lo), core: 2. Of those that a mesh axis runs over, the one named last changes fastest.
Arguments:
- values: bfloat16 [65536, 1024], P('seq', 'chan'), may hold values from -6 to 6
- inner_gate: bfloat16 [65536, 1024], P('seq', 'chan'), may hold values from -6 to 6
- outer_gate: bfloat16 [65536, 1024], P('seq', 'chan'), may hold values from -6 to 6
- filters: bfloat16 [65536, 64], P('seq', 'chan'), may hold values from -1.1 to 1.1
- skip: float32 [1024], P('chan'), may hold values from -4 to 4
- w_out: bfloat16 [1024, 1024], replicated, may hold values from -0.1875 to 0.1875
Outputs:
- mixed: bfloat16 [65536, 1024], P('seq', 'chan')
All inputs are finite; a program needn't handle non-finite values.
Results may differ from a plain program's by a relative error of at most 0.006.
Values may be sent and summed in bfloat16 or wider, within the bound.
A program may use at most 128 MiB of HBM per device.

v0:
```python
import math

import jax
import jax.numpy as jnp
from jax import lax
from jax.sharding import PartitionSpec as P

R = 32


highest_mode = lax.Precision.HIGHEST


def angle_table(left_index, right_index, whole_size, sign):
    product = left_index[:, None] * right_index[None, :] % whole_size
    angle = product.astype(jnp.float32) * (2.0 * math.pi / whole_size)
    return (jnp.cos(angle), sign * jnp.sin(angle))


def complex_einsum(form, real_part, imag_part, table_real, table_imag):
    first = jnp.einsum(form, real_part, table_real, precision=highest_mode)
    second = jnp.einsum(form, real_part, table_imag, precision=highest_mode)
    if imag_part is None:
        return (first, second)
    first = first - jnp.einsum(form, imag_part, table_imag, precision=highest_mode)
    second = second + jnp.einsum(form, imag_part, table_real, precision=highest_mode)
    return (first, second)


def complex_scale(real_part, imag_part, table_real, table_imag):
    return (
        real_part * table_real - imag_part * table_imag,
        real_part * table_imag + imag_part * table_real,
    )


def monarch_pass(real_part, imag_part, radix_size, sign):
    block_count, span_size, width = real_part.shape
    shaped = (block_count, radix_size, radix_size, width)
    small_index = jnp.arange(radix_size, dtype=jnp.int32)
    small_real, small_imag = angle_table(small_index, small_index, radix_size, sign)
    twist_real, twist_imag = angle_table(small_index, small_index, span_size, sign)
    real_part, imag_part = complex_einsum(
        "kijx,io->kojx",
        real_part.reshape(shaped),
        imag_part.reshape(shaped),
        small_real,
        small_imag,
    )
    real_part, imag_part = complex_scale(
        real_part, imag_part, twist_real[None, :, :, None], twist_imag[None, :, :, None]
    )
    real_part, imag_part = complex_einsum(
        "kojx,jq->kqox", real_part, imag_part, small_real, small_imag
    )
    return (
        real_part.reshape(block_count, span_size, width),
        imag_part.reshape(block_count, span_size, width),
    )


def shards(values, inner_gate, outer_gate, filters, skip, w_out):
    seq_count = lax.axis_size("seq")
    seq_place = lax.axis_index("seq")
    length, channels = values.shape
    group_count = filters.shape[1]
    radix_size = R
    span_size = radix_size * radix_size
    half_count = length * seq_count // span_size
    full_count = 2 * half_count
    whole_size = full_count * span_size
    part_count = span_size // seq_count
    block_count = full_count // seq_count
    signal = (inner_gate.astype(jnp.float32) * values.astype(jnp.float32)).astype(jnp.bfloat16)
    moved_signal, moved_filter = (
        lax.all_to_all(
            signal.reshape(length // span_size, span_size, channels),
            "seq",
            split_axis=1,
            concat_axis=0,
            tiled=True,
        ),
        lax.all_to_all(
            filters.reshape(length // span_size, span_size, group_count),
            "seq",
            split_axis=1,
            concat_axis=0,
            tiled=True,
        ),
    )
    local_rows = seq_place * part_count + jnp.arange(part_count, dtype=jnp.int32)
    half_index = jnp.arange(half_count, dtype=jnp.int32)
    full_index = jnp.arange(full_count, dtype=jnp.int32)
    front_real, front_imag = angle_table(half_index, full_index, full_count, -1.0)
    twist_real, twist_imag = angle_table(full_index, local_rows, whole_size, -1.0)

    def forward_rows(real_part, imag_part):
        real_part, imag_part = complex_einsum(
            "npx,nk->kpx", real_part, imag_part, front_real, front_imag
        )
        return complex_scale(real_part, imag_part, twist_real[:, :, None], twist_imag[:, :, None])

    signal_float = moved_signal.astype(jnp.float32)
    data_real, data_imag = forward_rows(signal_float, None)
    filter_real, filter_imag = forward_rows(moved_filter.astype(jnp.float32), None)
    data_real, data_imag, filter_real, filter_imag = (
        lax.all_to_all(data_real, "seq", split_axis=0, concat_axis=1, tiled=True),
        lax.all_to_all(data_imag, "seq", split_axis=0, concat_axis=1, tiled=True),
        lax.all_to_all(filter_real, "seq", split_axis=0, concat_axis=1, tiled=True),
        lax.all_to_all(filter_imag, "seq", split_axis=0, concat_axis=1, tiled=True),
    )
    data_real, data_imag = monarch_pass(data_real, data_imag, radix_size, -1.0)
    filter_real, filter_imag = monarch_pass(filter_real, filter_imag, radix_size, -1.0)
    width = data_real.shape[2]
    grouped = (block_count, span_size, group_count, width // group_count)
    data_real, data_imag = complex_scale(
        data_real.reshape(grouped),
        data_imag.reshape(grouped),
        filter_real[..., None],
        filter_imag[..., None],
    )
    data_real, data_imag = monarch_pass(
        data_real.reshape(block_count, span_size, width),
        data_imag.reshape(block_count, span_size, width),
        radix_size,
        1.0,
    )
    local_blocks = seq_place * block_count + jnp.arange(block_count, dtype=jnp.int32)
    span_index = jnp.arange(span_size, dtype=jnp.int32)
    back_real, back_imag = angle_table(local_blocks, span_index, whole_size, 1.0)
    data_real, data_imag = complex_scale(
        data_real, data_imag, back_real[:, :, None], back_imag[:, :, None]
    )
    data_real, data_imag = (
        lax.all_to_all(data_real, "seq", split_axis=1, concat_axis=0, tiled=True),
        lax.all_to_all(data_imag, "seq", split_axis=1, concat_axis=0, tiled=True),
    )
    rear_real, rear_imag = angle_table(full_index, half_index, full_count, 1.0)
    inverse_scale = 1.0 / whole_size
    conv_rows = (
        jnp.einsum("kpx,kn->npx", data_real, rear_real, precision=highest_mode)
        - jnp.einsum("kpx,kn->npx", data_imag, rear_imag, precision=highest_mode)
    ) * inverse_scale
    conv_rows = lax.all_to_all(
        conv_rows.astype(jnp.bfloat16), "seq", split_axis=0, concat_axis=1, tiled=True
    ).reshape(length, channels)
    gated = (
        outer_gate.astype(jnp.float32)
        * (conv_rows.astype(jnp.float32) + skip[None, :] * signal.astype(jnp.float32))
    ).astype(jnp.bfloat16)
    column_start = lax.axis_index("chan") * channels
    w_columns = lax.dynamic_slice_in_dim(w_out, column_start, channels, 1)
    mixed = jnp.dot(
        lax.all_gather(gated, "chan", axis=1, tiled=True),
        w_columns,
        preferred_element_type=jnp.float32,
    )
    return mixed.astype(jnp.bfloat16)


def solution(mesh):
    in_specs = (
        P("seq", "chan"),
        P("seq", "chan"),
        P("seq", "chan"),
        P("seq", "chan"),
        P("chan"),
        P(),
    )
    out_specs = P("seq", "chan")
    return jax.shard_map(shards, mesh=mesh, in_specs=in_specs, out_specs=out_specs, check_vma=False)
```

profile of v0, /device:TPU:2, one launch (start us, length us, event | category | flops | bytes accessed | tf_op | source)
XLA Modules:
  0.0 513.8 jit_solution(6303478593216569660)
XLA Ops:
  6.5 1.2 copy.98
  8.9 9.1 %all-to-all-start.3 = ((bf16[32,2,256]{2,1,0:T(2,128)(2,1)}), bf16[32,2,256]{2,1,0:T(2,128)(2,1)S(1)}, u32[]{:S(2)}, u32[]{:S(2)}) async-start(bf16[32,2,256]{2,1,0:T(2,128)(2,1)} %reshape.208), calls=%async_computation.3 | async-start | bytes 65536 | tf_op jit(solution)/shard_map/all_to_all | solution.py:83
  18.0 1.3 multiply_convert_fusion
  20.2 1.3 copy.89
  21.5 3.2 all-to-all-done.3
  24.7 5.0 all-to-all-start
  34.0 9.9 %all-to-all-done = bf16[2,1024,128]{2,0,1:T(2,128)(2,1)S(1)} async-done(((bf16[2,1024,128]{2,0,1:T(2,128)(2,1)}), bf16[2,1024,128]{2,0,1:T(2,128)(2,1)S(1)}, u32[]{:S(2)}, u32[]{:S(2)}) %all-to-all-start) | async-done | bytes 524320 | tf_op jit(solution)/shard_map/all_to_all | solution.py:76
  43.8 6.4 %all-to-all-start.4 = ((f32[32,1,1024]{2,1,0:T(1,128)}), f32[32,1,1024]{2,1,0:T(1,128)S(1)}, u32[]{:S(2)}, u32[]{:S(2)}) async-start(f32[32,1,1024]{2,1,0:T(1,128)} %reshape.210), calls=%async_computation.4 | async-start | bytes 262144 | tf_op jit(solution)/shard_map/all_to_all | solution.py:109
  50.9 2.5 fusion.84
  53.3 4.7 all-to-all-done.4
  58.0 5.0 all-to-all-start.5
  63.0 4.4 multiply_subtract_fusion
  67.3 2.6 copy.94
  70.7 7.0 %all-to-all-start.2 = ((f32[128,32,128]{2,1,0:T(8,128)}), f32[128,32,128]{2,1,0:T(8,128)}, u32[]{:S(2)}, u32[]{:S(2)}) async-start(f32[128,32,128]{2,1,0:T(8,128)} %copy.94), calls=%async_computation.2 | async-start | bytes 4194304 | tf_op jit(solution)/shard_map/all_to_all | solution.py:108
  77.7 4.1 copy.92
  81.8 43.9 %all-to-all-done.2 = f32[128,32,128]{2,1,0:T(8,128)} async-done(((f32[128,32,128]{2,1,0:T(8,128)}), f32[128,32,128]{2,1,0:T(8,128)}, u32[]{:S(2)}, u32[]{:S(2)}) %all-to-all-start.2) | async-done | bytes 2097184 | tf_op jit(solution)/shard_map/all_to_all | solution.py:108
  125.7 7.5 %all-to-all-start.1 = ((f32[128,32,128]{2,1,0:T(8,128)}), f32[128,32,128]{2,1,0:T(8,128)}, u32[]{:S(2)}, u32[]{:S(2)}) async-start(f32[128,32,128]{2,1,0:T(8,128)} %copy.92), calls=%async_computation.1 | async-start | bytes 4194304 | tf_op jit(solution)/shard_map/all_to_all | solution.py:107
  139.3 1.9 convolution_add_fusion.2
  141.2 2.5 fusion.56
  143.7 3.3 fusion.50
  147.0 1.3 mul.859
  148.3 1.6 mul.860
  149.9 6.5 %mul.861 = f32[4,32,32,128]{2,1,3,0:T(8,128)} reshape(f32[4,1024,8,16]{1,3,2,0:T(8,128)} %mul.860) | data formatting | bytes 4194304 | tf_op jit(solution)/shard_map/mul | solution.py:32
  156.4 8.0 %copy.112 = f32[4,32,32,128]{3,1,2,0:T(8,128)} copy(f32[4,32,32,128]{2,1,3,0:T(8,128)} %mul.861) | data formatting | bytes 4194304 | tf_op jit(solution)/shard_map/mul | solution.py:32
  164.4 2.5 fusion.58
  166.9 3.3 fusion.51
  170.2 1.3 mul.855
  171.5 1.6 mul.856
  173.1 6.5 %mul.857 = f32[4,32,32,128]{2,1,3,0:T(8,128)} reshape(f32[4,1024,8,16]{1,3,2,0:T(8,128)} %mul.856) | data formatting | bytes 4194304 | tf_op jit(solution)/shard_map/mul | solution.py:32
  179.6 8.3 %copy.109 = f32[4,32,32,128]{3,1,2,0:T(8,128)} copy(f32[4,32,32,128]{2,1,3,0:T(8,128)} %mul.857) | data formatting | bytes 4194304 | tf_op jit(solution)/shard_map/mul | solution.py:32
  187.9 5.9 %fusion.6 = f32[32,4,32,128]{3,0,2,1:T(8,128)} fusion(f32[32,4,32,128]{3,2,1,0:T(8,128)} %bitcast.14), kind=kOutput, calls=%fused_computation.15 | convolution fusion | flops 201341952 | bytes 4194304 | tf_op jit(solution)/shard_map/kijx,io->kojx/dot_general | solution.py:25
  193.9 5.9 %fusion.4 = f32[32,4,32,128]{3,0,2,1:T(8,128)} fusion(f32[32,4,32,128]{3,2,1,0:T(8,128)} %bitcast.14), kind=kOutput, calls=%fused_computation.13 | convolution fusion | flops 201340928 | bytes 4194304 | tf_op jit(solution)/shard_map/kijx,io->kojx/dot_general | solution.py:26
  199.7 5.4 %fusion.42 = f32[32,4,32,128]{3,0,2,1:T(8,128)S(1)} fusion(f32[32,4,32,128]{3,0,2,1:T(8,128)} %fusion.6, f32[32,4,32,128]{3,2,1,0:T(8,128)} %bitcast.10), kind=kOutput, calls=%fused_computation.51 | convolution fusion | flops 201865216 | bytes 6291456 | tf_op jit(solution)/shard_map/kijx,io->kojx/dot_general | solution.py:21
  205.2 5.5 %subtract_bitcast_fusion.2 = (f32[4,32,32,128]{3,1,2,0:T(8,128)S(1)}, f32[4,32,32,128]{3,1,2,0:T(8,128)S(1)}) fusion(f32[32,4,32,128]{3,0,2,1:T(8,128)S(1)} %fusion.42, f32[32,32]{0,1:T(8,128)S(1)} %get-tuple-element.21, f32[32,32]{0,1:T(8,128)S(1)} %get-tuple-element.22, f32[32,4,32,128]{3,0,2,1:T(8,128)S(1)} %copy-done.3, f32[32,4,32,128]{3,2,1,0:T(8,128)} %bitcast.10), kind=kOutput, calls=%fused_computation.26 | convolution fusion | flops 205011968 | bytes 10493952 | tf_op jit(solution)/shard_map/kijx,io->kojx/dot_general | solution.py:22
  210.7 3.0 fusion.22
  213.7 3.0 fusion.20
  216.8 3.0 fusion.32
  219.8 3.8 fusion.3
  223.6 1.9 fusion.108
  225.5 1.9 fusion.122
  227.5 1.9 convolution_add_fusion
  229.4 2.5 subtract_bitcast_fusion.1
  231.9 3.5 fusion.14
  235.4 3.0 fusion.12
  238.5 3.1 subtract_bitcast_fusion
  241.6 1.2 copy.117
  242.8 3.1 add_bitcast_fusion
  245.9 1.2 copy.120
  247.1 2.8 fusion.1
  249.9 2.7 copy.121
  252.7 7.8 %all-to-all-start.6 = ((f32[4,1024,128]{2,0,1:T(4,128)}), f32[4,1024,128]{2,0,1:T(4,128)}, u32[]{:S(2)}, u32[]{:S(2)}) async-start(f32[4,1024,128]{2,0,1:T(4,128)} %copy.121), calls=%async_computation.6 | async-start | bytes 4194304 | tf_op jit(solution)/shard_map/all_to_all | solution.py:135
  260.5 4.3 copy.124
  264.8 43.7 %all-to-all-done.6 = f32[4,1024,128]{2,0,1:T(4,128)} async-done(((f32[4,1024,128]{2,0,1:T(4,128)}), f32[4,1024,128]{2,0,1:T(4,128)}, u32[]{:S(2)}, u32[]{:S(2)}) %all-to-all-start.6) | async-done | bytes 2097184 | tf_op jit(solution)/shard_map/all_to_all | solution.py:135
  308.5 7.1 %all-to-all-start.7 = ((f32[4,1024,128]{2,0,1:T(4,128)}), f32[4,1024,128]{2,0,1:T(4,128)}, u32[]{:S(2)}, u32[]{:S(2)}) async-start(f32[4,1024,128]{2,0,1:T(4,128)} %copy.124), calls=%async_computation.7 | async-start | bytes 4194304 | tf_op jit(solution)/shard_map/all_to_all | solution.py:136
  315.7 1.7 copy.122
  317.4 1.4 copy.123
  318.8 1.3 fusion.86
  320.1 43.5 %all-to-all-done.7 = f32[4,1024,128]{2,0,1:T(4,128)} async-done(((f32[4,1024,128]{2,0,1:T(4,128)}), f32[4,1024,128]{2,0,1:T(4,128)}, u32[]{:S(2)}, u32[]{:S(2)}) %all-to-all-start.7) | async-done | bytes 2097184 | tf_op jit(solution)/shard_map/all_to_all | solution.py:136
  363.6 1.7 copy.125
  365.3 1.4 copy.126
  366.6 1.3 fusion.49
  368.4 20.4 %all_to_all.141 = bf16[64,32,128]{2,1,0:T(8,128)(2,1)S(1)} all-to-all(bf16[64,32,128]{2,1,0:T(8,128)(2,1)S(1)} %copy.127), channel_id=1, replica_groups=mesh['seq'=32,'chan'=8] {'seq'}, dimensions={0} | all-to-all | bytes 1048576 | tf_op jit(solution)/shard_map/all_to_all | solution.py:144
  390.0 112.5 %all-gather.2.cloned.1.call-done = bf16[2048,1024]{1,0:T(8,128)(2,1)} async-done(((bf16[2048,128]{1,0:T(8,128)(2,1)}), bf16[2048,1024]{1,0:T(8,128)(2,1)}) %all-gather.2.cloned.1.call-update) | async-done | bytes 4194320 | tf_op jit(solution)/shard_map/all_gather | solution.py:154
  502.5 4.2 convolution_convert_fusion
  (53 shorter events, 15.2 us)
Async XLA Ops:
  6.5 496.0 %copy-start = (bf16[1024,1024]{1,0:T(8,128)(2,1)S(1)}, bf16[1024,1024]{1,0:T(8,128)(2,1)}, u32[]{:S(2)}) copy-start(bf16[1024,1024]{1,0:T(8,128)(2,1)} %param.11) | copy-start | bytes 6291460
  8.9 15.7 %all-to-all-start.3 = ((bf16[32,2,256]{2,1,0:T(2,128)(2,1)}), bf16[32,2,256]{2,1,0:T(2,128)(2,1)S(1)}, u32[]{:S(2)}, u32[]{:S(2)}) async-start(bf16[32,2,256]{2,1,0:T(2,128)(2,1)} %reshape.208), calls=%async_computation.3 | async-start | bytes 65536 | tf_op jit(solution)/shard_map/all_to_all | solution.py:83
  19.3 0.8 copy-start.5
  24.7 19.2 %all-to-all-start = ((bf16[2,1024,128]{2,0,1:T(2,128)(2,1)}), bf16[2,1024,128]{2,0,1:T(2,128)(2,1)S(1)}, u32[]{:S(2)}, u32[]{:S(2)}) async-start(bf16[2,1024,128]{2,0,1:T(2,128)(2,1)} %copy.89), calls=%async_computation | async-start | bytes 1048576 | tf_op jit(solution)/shard_map/all_to_all | solution.py:76
  43.8 14.2 %all-to-all-start.4 = ((f32[32,1,1024]{2,1,0:T(1,128)}), f32[32,1,1024]{2,1,0:T(1,128)S(1)}, u32[]{:S(2)}, u32[]{:S(2)}) async-start(f32[32,1,1024]{2,1,0:T(1,128)} %reshape.210), calls=%async_computation.4 | async-start | bytes 262144 | tf_op jit(solution)/shard_map/all_to_all | solution.py:109
  58.0 12.7 %all-to-all-start.5 = ((f32[32,1,1024]{2,1,0:T(1,128)}), f32[32,1,1024]{2,1,0:T(1,128)S(1)}, u32[]{:S(2)}, u32[]{:S(2)}) async-start(f32[32,1,1024]{2,1,0:T(1,128)} %reshape.212), calls=%async_computation.5 | async-start | bytes 262144 | tf_op jit(solution)/shard_map/all_to_all | solution.py:110
  70.7 55.0 %all-to-all-start.2 = ((f32[128,32,128]{2,1,0:T(8,128)}), f32[128,32,128]{2,1,0:T(8,128)}, u32[]{:S(2)}, u32[]{:S(2)}) async-start(f32[128,32,128]{2,1,0:T(8,128)} %copy.94), calls=%async_computation.2 | async-start | bytes 4194304 | tf_op jit(solution)/shard_map/all_to_all | solution.py:108
  125.7 74.0 %all-to-all-start.1 = ((f32[128,32,128]{2,1,0:T(8,128)}), f32[128,32,128]{2,1,0:T(8,128)}, u32[]{:S(2)}, u32[]{:S(2)}) async-start(f32[128,32,128]{2,1,0:T(8,128)} %copy.92), calls=%async_computation.1 | async-start | bytes 4194304 | tf_op jit(solution)/shard_map/all_to_all | solution.py:107
  136.5 1.8 copy-start.4
  199.7 5.4 %copy-start.3 = (f32[32,4,32,128]{3,0,2,1:T(8,128)S(1)}, f32[32,4,32,128]{3,0,2,1:T(8,128)}, u32[]{:S(2)}) copy-start(f32[32,4,32,128]{3,0,2,1:T(8,128)} %fusion.4) | copy-start | bytes 6291460
  216.7 3.0 copy-start.1
  216.8 3.0 copy-start.2
  252.7 55.8 %all-to-all-start.6 = ((f32[4,1024,128]{2,0,1:T(4,128)}), f32[4,1024,128]{2,0,1:T(4,128)}, u32[]{:S(2)}, u32[]{:S(2)}) async-start(f32[4,1024,128]{2,0,1:T(4,128)} %copy.121), calls=%async_computation.6 | async-start | bytes 4194304 | tf_op jit(solution)/shard_map/all_to_all | solution.py:135
  308.5 55.1 %all-to-all-start.7 = ((f32[4,1024,128]{2,0,1:T(4,128)}), f32[4,1024,128]{2,0,1:T(4,128)}, u32[]{:S(2)}, u32[]{:S(2)}) async-start(f32[4,1024,128]{2,0,1:T(4,128)} %copy.124), calls=%async_computation.7 | async-start | bytes 4194304 | tf_op jit(solution)/shard_map/all_to_all | solution.py:136
  315.6 186.9 %all-gather.2.cloned.1.call-start = ((), (), s32[]{:S(2)}) async-start(), calls=%async_computation.9 | async-start | bytes 4718592 | tf_op jit(solution)/shard_map/all_gather | solution.py:154
  368.0 20.9 %copy-start.6 = (bf16[2048,128]{1,0:T(8,128)(2,1)S(1)}, bf16[2048,128]{1,0:T(8,128)(2,1)}, u32[]{:S(2)}) copy-start(bf16[2048,128]{1,0:T(8,128)(2,1)} %copy-done.5) | copy-start | bytes 1572868
  368.0 20.9 %copy-start.7 = (bf16[2048,128]{1,0:T(8,128)(2,1)S(1)}, bf16[2048,128]{1,0:T(8,128)(2,1)}, u32[]{:S(2)}) copy-start(bf16[2048,128]{1,0:T(8,128)(2,1)} %param.8) | copy-start | bytes 1572868
  368.0 20.9 %copy-start.8 = (f32[128]{0:T(128)S(1)}, f32[128]{0:T(128)}, u32[]{:S(2)}) copy-start(f32[128]{0:T(128)} %param.10) | copy-start | bytes 1540
Sparse Core Ops, SparseCore 0:
  390.1 112.3 all-gather.1
where the time goes:
time: 524 us; the launch traced here: 514 us
  waiting for transfers between devices  262 us (50%)
  matrix products  87.2 us (17%)
  local copies, waits for them, and re-layouts  67.4 us (13%)
  starting transfers between devices  54.9 us (10%)
  blocking collectives  20.4 us (4%)
  between operations  14.1 us (3%)
  other arithmetic  7.67 us (1%)
    all_gather x1, waiting for transfers between devices, shards(): lax.all_gather(gated, 'chan', axis=1, tiled=True)  113 us
    all_to_all x1, waiting for transfers between devices, shards(): lax.all_to_all(data_imag, 'seq', split_axis=0, concat_axis=1, tiled=True)  43.9 us
    all_to_all x1, waiting for transfers between devices, shards(): lax.all_to_all(data_real, 'seq', split_axis=1, concat_axis=0, tiled=True)  43.7 us
    all_to_all x1, waiting for transfers between devices, shards(): lax.all_to_all(data_imag, 'seq', split_axis=1, concat_axis=0, tiled=True)  43.5 us
    dot_general x8, matrix products, complex_einsum(): second = jnp.einsum(form, real_part, table_imag, precision=highest_mode)  22.4 us
    all_to_all x1, blocking collectives, shards(): lax.all_to_all(conv_rows.astype(jnp.bfloat16), 'seq', split_axis=0, conca...  20.4 us
    dot_general x8, matrix products, complex_einsum(): first = jnp.einsum(form, real_part, table_real, precision=highest_mode)  19.7 us
    dot_general x6, matrix products, complex_einsum(): jnp.einsum(form, imag_part, table_imag, precision=highest_mode)  19.1 us
  transfers between devices with their start and end apart: 9, of which 8 were waited for; matrix products, arithmetic and copies ran while one was open for 19% of the time, Pallas kernels for 0%

commit v1 on v0

v1 whole, which is shorter than its diff:
```python
import functools

import jax
import jax.numpy as jnp
import numpy as np
from jax import lax
from jax.experimental import pallas as pl
from jax.experimental.pallas import tpu as pltpu
from jax.sharding import PartitionSpec as P

F32 = jnp.float32
BF16 = jnp.bfloat16
LANES = 128
ROWS = 512
CHUNK = 256


def split_table(table):
    high = table.astype(jnp.bfloat16)
    low = (table - high.astype(np.float64)).astype(jnp.bfloat16)
    return high, low


@functools.lru_cache(maxsize=None)
def tables(rows):
    n = rows * LANES
    quarter = 4 * np.arange(rows, dtype=np.int64) + 1
    first = np.arange(rows, dtype=np.int64)
    angle = 2.0 * np.pi * ((quarter[:, None] * first[None, :]) % (4 * rows)) / (4 * rows)
    front = np.concatenate([np.cos(angle), -np.sin(angle)], axis=0)
    lane = np.arange(LANES, dtype=np.int64)
    angle = 2.0 * np.pi * (quarter[:, None] * lane[None, :]) / (4 * n)
    twist_real = np.cos(angle).astype(np.float32)
    twist_imag = (-np.sin(angle)).astype(np.float32)
    angle = 2.0 * np.pi * ((lane[:, None] * lane[None, :]) % LANES) / LANES
    cos, sin = np.cos(angle), np.sin(angle)
    mid = np.block([[cos, -sin], [sin, cos]])
    back = np.block([[cos, sin], [-sin, cos]])
    return (
        *split_table(front),
        *split_table(front.T / n),
        *split_table(mid),
        *split_table(back),
        twist_real,
        twist_imag,
    )


def halves(value):
    high = value.astype(BF16)
    return high, (value - high.astype(F32)).astype(BF16)


def dot(left, right):
    return jnp.dot(left, right, preferred_element_type=F32)


def dot3(left, right_high, right_low):
    left_high, left_low = halves(left)
    return dot(left_high, right_high) + (dot(left_high, right_low) + dot(left_low, right_high))


def pack_kernel(values_ref, inner_ref, filters_ref, out_ref, wide_ref, wide_filter_ref):
    parts = out_ref.shape[0]
    tiles = values_ref.shape[0] // LANES
    channels = values_ref.shape[1]
    groups = filters_ref.shape[1]
    for tile in range(tiles):
        rows = pl.ds(tile * LANES, LANES)
        signal = inner_ref[rows, :].astype(F32) * values_ref[rows, :].astype(F32)
        wide_ref[pl.ds(tile, channels, stride=tiles), :] = signal.T
        wide_filter_ref[pl.ds(tile, groups, stride=tiles), :] = filters_ref[rows, :].astype(F32).T
    own = channels // parts * tiles
    out_ref[:, :own, :] = wide_ref[...].astype(BF16).reshape(parts, own, LANES)
    for part in range(parts):
        group = part * groups // parts
        out_ref[part, own:, :] = wide_filter_ref[pl.ds(group * tiles, tiles), :].astype(BF16)


def conv_kernel(
    moved_ref,
    front_high,
    front_low,
    rear_high,
    rear_low,
    mid_high,
    mid_low,
    back_high,
    back_low,
    twist_real,
    twist_imag,
    out_ref,
    data_ref,
    filter_ref,
    high_ref,
    low_ref,
):
    parts, packed, _ = moved_ref.shape
    tiles = ROWS // parts
    count = packed // tiles - 1
    for part in range(parts):
        rows = pl.ds(part * tiles, tiles)
        for channel in range(count):
            data_ref[rows, pl.ds(channel * LANES, LANES)] = moved_ref[
                part, pl.ds(channel * tiles, tiles), :
            ]
        filter_ref[rows, :] = moved_ref[part, pl.ds(count * tiles, tiles), :]

    def forward(columns, rows):
        return dot(front_high[rows, :], columns) + dot(front_low[rows, :], columns)

    def chunk_step(step, carry):
        start = pl.multiple_of(step * CHUNK, CHUNK)
        real_rows = pl.ds(start, CHUNK)
        imag_rows = pl.ds(pl.multiple_of(start + ROWS, CHUNK), CHUNK)
        turn_real, turn_imag = twist_real[real_rows, :], twist_imag[real_rows, :]

        def spectrum(real, imag):
            turned = jnp.concatenate(
                [real * turn_real - imag * turn_imag, real * turn_imag + imag * turn_real], axis=1
            )
            both = dot3(turned, mid_high[...], mid_low[...])
            return both[:, :LANES], both[:, LANES:]

        kernel = filter_ref[...]
        kernel_real, kernel_imag = spectrum(forward(kernel, real_rows), forward(kernel, imag_rows))
        data = data_ref[...]
        all_real, all_imag = forward(data, real_rows), forward(data, imag_rows)
        for channel in range(count):
            lanes = pl.ds(channel * LANES, LANES)
            real, imag = spectrum(
                all_real[:, channel * LANES : (channel + 1) * LANES],
                all_imag[:, channel * LANES : (channel + 1) * LANES],
            )
            product = jnp.concatenate(
                [
                    real * kernel_real - imag * kernel_imag,
                    real * kernel_imag + imag * kernel_real,
                ],
                axis=1,
            )
            both = dot3(product, back_high[...], back_low[...])
            real, imag = both[:, :LANES], both[:, LANES:]
            high, low = halves(real * turn_real + imag * turn_imag)
            high_ref[real_rows, lanes], low_ref[real_rows, lanes] = high, low
            high, low = halves(imag * turn_real - real * turn_imag)
            high_ref[imag_rows, lanes], low_ref[imag_rows, lanes] = high, low
        return carry

    lax.fori_loop(0, ROWS // CHUNK, chunk_step, 0)

    def rear_step(step, carry):
        rows = pl.ds(pl.multiple_of(step * CHUNK, CHUNK), CHUNK)
        high, low = high_ref[...], low_ref[...]
        result = dot(rear_high[rows, :], high) + (
            dot(rear_low[rows, :], high) + dot(rear_high[rows, :], low)
        )
        result = result.astype(BF16)
        own = CHUNK // tiles
        for channel in range(count):
            out_ref[pl.ds(step * own, own), pl.ds(channel * tiles, tiles), :] = result[
                :, channel * LANES : (channel + 1) * LANES
            ].reshape(own, tiles, LANES)
        return carry

    lax.fori_loop(0, ROWS // CHUNK, rear_step, 0)


def gate_kernel(moved_ref, values_ref, inner_ref, outer_ref, skip_ref, out_ref, wide_ref):
    tiles = values_ref.shape[0] // LANES
    channels = values_ref.shape[1]
    wide_ref[...] = moved_ref[...].astype(F32).reshape(wide_ref.shape)
    for tile in range(tiles):
        rows = pl.ds(tile * LANES, LANES)
        conv = wide_ref[pl.ds(tile, channels, stride=tiles), :].T
        signal = inner_ref[rows, :].astype(F32) * values_ref[rows, :].astype(F32)
        signal = signal.astype(BF16).astype(F32)
        gated = outer_ref[rows, :].astype(F32) * (conv + skip_ref[...] * signal)
        out_ref[rows, :] = gated.astype(BF16)


def mix_kernel(gated_ref, weight_ref, out_ref):
    parts, _, width = gated_ref.shape
    joined = jnp.concatenate([gated_ref[part] for part in range(parts)], axis=1)
    for part in range(0, parts, 2):
        mixed = dot(joined, weight_ref[:, pl.ds(part * width, 2 * width)]).astype(BF16)
        out_ref[part] = mixed[:, :width]
        out_ref[part + 1] = mixed[:, width:]


def call(kernel, shape, scratch=(), flops=0):
    return pl.pallas_call(
        kernel,
        out_shape=jax.ShapeDtypeStruct(shape, BF16),
        scratch_shapes=list(scratch),
        compiler_params=pltpu.CompilerParams(vmem_limit_bytes=48 << 20),
        cost_estimate=pl.CostEstimate(flops=flops, bytes_accessed=2 << 20, transcendentals=0),
    )


def shards(values, inner_gate, outer_gate, filters, skip, w_out):
    parts = lax.axis_size("seq")
    ranks = lax.axis_size("chan")
    length, channels = values.shape
    groups = filters.shape[1]
    tiles = length // LANES
    count = channels // parts
    packed = call(
        pack_kernel,
        (parts, (count + 1) * tiles, LANES),
        [pltpu.VMEM((channels * tiles, LANES), F32), pltpu.VMEM((groups * tiles, LANES), F32)],
    )(values, inner_gate, filters)
    moved = lax.all_to_all(packed, "seq", split_axis=0, concat_axis=0, tiled=True)
    conv = call(
        conv_kernel,
        (parts, count * tiles, LANES),
        [
            pltpu.VMEM((ROWS, count * LANES), BF16),
            pltpu.VMEM((ROWS, LANES), BF16),
            pltpu.VMEM((2 * ROWS, count * LANES), BF16),
            pltpu.VMEM((2 * ROWS, count * LANES), BF16),
        ],
        flops=5 * 10**9,
    )(moved, *[jnp.asarray(table) for table in tables(ROWS)])
    conv = lax.all_to_all(conv, "seq", split_axis=0, concat_axis=0, tiled=True)
    gated = call(gate_kernel, (length, channels), [pltpu.VMEM((channels * tiles, LANES), F32)])(
        conv, values, inner_gate, outer_gate, skip[None, :]
    )
    shape = (ranks, length // ranks, channels)
    gated = lax.all_to_all(gated.reshape(shape), "chan", split_axis=0, concat_axis=0, tiled=True)
    mixed = call(mix_kernel, shape, flops=2 * length * channels * channels * ranks)(gated, w_out)
    mixed = lax.all_to_all(mixed, "chan", split_axis=0, concat_axis=0, tiled=True)
    return mixed.reshape(length, channels)


def solution(mesh):
    in_specs = (
        P("seq", "chan"),
        P("seq", "chan"),
        P("seq", "chan"),
        P("seq", "chan"),
        P("chan"),
        P(),
    )
    out_specs = P("seq", "chan")
    return jax.shard_map(shards, mesh=mesh, in_specs=in_specs, out_specs=out_specs, check_vma=False)
```

time: 524 us -> 110 us (0.21)
  the two profiles are of different devices: /device:TPU:2 before, /device:TPU:33 now
where the time goes in v1:
time: 110 us; the launch traced here: 109 us
  blocking collectives  94.3 us (86%)
  Pallas kernels  10.2 us (9%)
  local copies, waits for them, and re-layouts  4.91 us (4%)
    all_to_all x1, blocking collectives, shards(): lax.all_to_all(gated.reshape(shape), 'chan', split_axis=0, concat_axis=0,...  26.8 us
    all_to_all x1, blocking collectives, shards(): lax.all_to_all(packed, 'seq', split_axis=0, concat_axis=0, tiled=True)  25.4 us
    all_to_all x1, blocking collectives, shards(): lax.all_to_all(mixed, 'chan', split_axis=0, concat_axis=0, tiled=True)  21.3 us
    all_to_all x1, blocking collectives, shards(): conv = lax.all_to_all(conv, 'seq', split_axis=0, concat_axis=0, tiled=True)  20.8 us
    pallas_call x1, Pallas kernels, shards(): call(conv_kernel, (parts, count * tiles, LANES), [pltpu.VMEM((ROWS, count...  8.31 us
    unnamed x34, local copies, waits for them, and re-layouts  4.91 us

profile of v1, /device:TPU:33, one launch (start us, length us, event | category | flops | bytes accessed | tf_op | source)
XLA Modules:
  0.0 109.5 jit_solution(2611802235666601583)
XLA Ops:
  0.0 0.0 copy-start.10
  0.0 0.0 copy-start.11
  0.0 1.1 copy.17.filters_ref
  1.1 0.0 copy-start.1
  1.1 1.0 copy-done.1
  2.1 0.0 copy-start.3
  2.1 1.0 copy-done.3
  3.2 0.0 copy-start.7
  3.2 0.0 copy-start.8
  3.2 0.0 copy-start.9
  3.2 0.0 copy-start.12
  3.2 0.0 copy-start.13
  3.2 0.0 copy-start.14
  3.2 0.6 shard_map.154
  3.8 25.4 %all_to_all.20.moved_ref = bf16[32,80,128]{2,1,0:T(8,128)(2,1)S(1)} all-to-all(bf16[32,80,128]{2,1,0:T(8,128)(2,1)S(1)} %shard_map.154), channel_id=1, replica_groups=mesh['seq'=32,'chan'=8] {'seq'}, dimensions={0} | all-to-all | bytes 1310720 | tf_op jit(solution)/shard_map/all_to_all | solution.py:213
  29.2 0.0 copy-done.10
  29.3 0.0 copy-done.11
  29.3 0.0 copy-done.7
  29.3 0.0 copy-done.8
  29.3 0.0 copy-done.9
  29.3 0.0 copy-done.12
  29.3 0.0 copy-done.13
  29.3 0.0 copy-done.14
  29.3 0.0 copy-start.15
  29.3 0.9 copy-done.15
  30.2 0.0 copy-start.2
  30.2 0.0 copy-start.4
  30.2 0.0 copy-start.5
  30.2 0.0 copy-start.6
  30.2 8.3 %shard_map.155 = bf16[32,64,128]{2,1,0:T(8,128)(2,1)S(1)} custom-call(bf16[32,80,128]{2,1,0:T(8,128)(2,1)S(1)} %all_to_all.20.moved_ref, bf16[1024,512]{1,0:T(8,128)(2,1)S(1)} %copy-done.9, bf16[1024,512]{1,0:T(8,128)(2,1)S(1)} %copy-done.8, bf16[512,1024]{1,0:T(8,128)(2,1)S(1)} %copy-done.7, bf16[512,1024]{1,0:T(8,128)(2,1)} %constant.23.clone.rear_low, ...), custom_call_target="tpu_custom_call" | custom-call | flops 5000000000 | bytes 2097152 | tf_op jit(solution)/shard_map/pallas_call | solution.py:214
  38.5 20.8 %all_to_all.21.moved_ref = bf16[32,64,128]{2,1,0:T(8,128)(2,1)S(1)} all-to-all(bf16[32,64,128]{2,1,0:T(8,128)(2,1)S(1)} %shard_map.155), channel_id=1, replica_groups=mesh['seq'=32,'chan'=8] {'seq'}, dimensions={0} | all-to-all | bytes 1048576 | tf_op jit(solution)/shard_map/all_to_all | solution.py:225
  59.4 0.0 copy-start
  59.4 0.0 copy-done.2
  59.4 0.0 copy-done.4
  59.4 0.0 copy-done.5
  59.4 0.0 copy-done.6
  59.4 0.5 shard_map.156
  59.9 26.8 %all_to_all.22.gated_ref = bf16[8,256,128]{2,1,0:T(8,128)(2,1)S(1)} all-to-all(bf16[8,256,128]{2,1,0:T(8,128)(2,1)S(1)} %bitcast.3), channel_id=1, replica_groups=mesh['seq'=32,'chan'=8] {'chan'}, dimensions={0} | all-to-all | bytes 1048576 | tf_op jit(solution)/shard_map/all_to_all | solution.py:230
  86.7 0.0 copy-done
  86.7 0.7 shard_map.157
  87.4 21.3 %all_to_all.23 = bf16[8,256,128]{2,1,0:T(8,128)(2,1)S(1)} all-to-all(bf16[8,256,128]{2,1,0:T(8,128)(2,1)S(1)} %shard_map.157), channel_id=1, replica_groups=mesh['seq'=32,'chan'=8] {'chan'}, dimensions={0} | all-to-all | bytes 1048576 | tf_op jit(solution)/shard_map/all_to_all | solution.py:232
  108.7 0.8 copy.19
Async XLA Ops:
  0.0 29.2 %copy-start.10 = (f32[512,128]{1,0:T(8,128)S(1)}, f32[512,128]{1,0:T(8,128)}, u32[]{:S(2)}) copy-start(f32[512,128]{1,0:T(8,128)} %constant.29.clone.twist_imag) | copy-start | bytes 786436
  0.0 29.3 %copy-start.11 = (f32[512,128]{1,0:T(8,128)S(1)}, f32[512,128]{1,0:T(8,128)}, u32[]{:S(2)}) copy-start(f32[512,128]{1,0:T(8,128)} %constant.28.clone.twist_real) | copy-start | bytes 786436
  1.1 1.0 copy-start.1
  2.1 1.0 copy-start.3
  3.2 26.1 %copy-start.7 = (bf16[512,1024]{1,0:T(8,128)(2,1)S(1)}, bf16[512,1024]{1,0:T(8,128)(2,1)}, u32[]{:S(2)}) copy-start(bf16[512,1024]{1,0:T(8,128)(2,1)} %constant.22.clone.rear_high) | copy-start | bytes 3145732
  3.2 26.1 %copy-start.8 = (bf16[1024,512]{1,0:T(8,128)(2,1)S(1)}, bf16[1024,512]{1,0:T(8,128)(2,1)}, u32[]{:S(2)}) copy-start(bf16[1024,512]{1,0:T(8,128)(2,1)} %constant.21.clone.front_low) | copy-start | bytes 3145732
  3.2 26.1 %copy-start.9 = (bf16[1024,512]{1,0:T(8,128)(2,1)S(1)}, bf16[1024,512]{1,0:T(8,128)(2,1)}, u32[]{:S(2)}) copy-start(bf16[1024,512]{1,0:T(8,128)(2,1)} %constant.20.clone.front_high) | copy-start | bytes 3145732
  3.2 26.1 %copy-start.12 = (bf16[256,256]{1,0:T(8,128)(2,1)S(1)}, bf16[256,256]{1,0:T(8,128)(2,1)}, u32[]{:S(2)}) copy-start(bf16[256,256]{1,0:T(8,128)(2,1)} %constant.27.clone.back_low) | copy-start | bytes 393220
  3.2 26.1 %copy-start.13 = (bf16[256,256]{1,0:T(8,128)(2,1)S(1)}, bf16[256,256]{1,0:T(8,128)(2,1)}, u32[]{:S(2)}) copy-start(bf16[256,256]{1,0:T(8,128)(2,1)} %constant.26.clone.back_high) | copy-start | bytes 393220
  3.2 26.1 %copy-start.14 = (bf16[256,256]{1,0:T(8,128)(2,1)S(1)}, bf16[256,256]{1,0:T(8,128)(2,1)}, u32[]{:S(2)}) copy-start(bf16[256,256]{1,0:T(8,128)(2,1)} %constant.25.clone.mid_low) | copy-start | bytes 393220
  29.3 0.9 copy-start.15
  30.2 29.2 %copy-start.2 = (bf16[2048,128]{1,0:T(8,128)(2,1)S(1)}, bf16[2048,128]{1,0:T(8,128)(2,1)}, u32[]{:S(2)}) copy-start(bf16[2048,128]{1,0:T(8,128)(2,1)} %values_ref.3) | copy-start | bytes 1572868
  30.2 29.2 %copy-start.4 = (bf16[2048,128]{1,0:T(8,128)(2,1)S(1)}, bf16[2048,128]{1,0:T(8,128)(2,1)}, u32[]{:S(2)}) copy-start(bf16[2048,128]{1,0:T(8,128)(2,1)} %inner_ref.3) | copy-start | bytes 1572868
  30.2 29.2 %copy-start.5 = (bf16[2048,128]{1,0:T(8,128)(2,1)S(1)}, bf16[2048,128]{1,0:T(8,128)(2,1)}, u32[]{:S(2)}) copy-start(bf16[2048,128]{1,0:T(8,128)(2,1)} %outer_ref.1) | copy-start | bytes 1572868
  30.2 29.2 %copy-start.6 = (f32[128]{0:T(128)S(1)}, f32[128]{0:T(128)}, u32[]{:S(2)}) copy-start(f32[128]{0:T(128)} %param.20) | copy-start | bytes 1540
  59.4 27.3 %copy-start = (bf16[1024,1024]{1,0:T(8,128)(2,1)S(1)}, bf16[1024,1024]{1,0:T(8,128)(2,1)}, u32[]{:S(2)}) copy-start(bf16[1024,1024]{1,0:T(8,128)(2,1)} %weight_ref.1) | copy-start | bytes 6291460

commit v2 on v1

v2 whole, which is shorter than its diff:
```python
import functools

import jax
import jax.numpy as jnp
import numpy as np
from jax import lax
from jax.experimental import pallas as pl
from jax.experimental.pallas import tpu as pltpu
from jax.sharding import PartitionSpec as P

F32 = jnp.float32
BF16 = jnp.bfloat16
MESH = pl.DeviceIdType.MESH
LANES = 128
STAGES = 2


def split_table(table):
    high = table.astype(jnp.bfloat16)
    low = (table - high.astype(np.float64)).astype(jnp.bfloat16)
    return high, low


@functools.lru_cache(maxsize=None)
def tables(rows):
    n = rows * LANES
    quarter = 4 * np.arange(rows, dtype=np.int64) + 1
    first = np.arange(rows, dtype=np.int64)
    angle = 2.0 * np.pi * ((quarter[:, None] * first[None, :]) % (4 * rows)) / (4 * rows)
    front = np.concatenate([np.cos(angle), -np.sin(angle)], axis=0)
    lane = np.arange(LANES, dtype=np.int64)
    angle = 2.0 * np.pi * (quarter[:, None] * lane[None, :]) / (4 * n)
    twist_real = np.cos(angle).astype(np.float32)
    twist_imag = (-np.sin(angle)).astype(np.float32)
    angle = 2.0 * np.pi * ((lane[:, None] * lane[None, :]) % LANES) / LANES
    cos, sin = np.cos(angle), np.sin(angle)
    mid = np.block([[cos, -sin], [sin, cos]])
    back = np.block([[cos, sin], [-sin, cos]])
    return (
        *split_table(front),
        *split_table(front.T / n),
        *split_table(mid),
        *split_table(back),
        twist_real,
        twist_imag,
    )


def halves(value):
    high = value.astype(BF16)
    return high, (value - high.astype(F32)).astype(BF16)


def dot(left, right):
    return jnp.dot(left, right, preferred_element_type=F32)


def dot3(left, right_high, right_low):
    left_high, left_low = halves(left)
    return dot(left_high, right_high) + (dot(left_high, right_low) + dot(left_low, right_high))


def wait_all(ref, sem):
    pltpu.make_async_copy(ref, ref, sem).wait()


def exchange(axis, me, size, send_ref, place_of, send_sem, recv_sem, prepare=None):
    def one(step, carry):
        other = lax.rem(me + step, size)
        if prepare is not None:
            prepare(other)
        pltpu.make_async_remote_copy(
            src_ref=send_ref.at[other],
            dst_ref=place_of(me),
            send_sem=send_sem,
            recv_sem=recv_sem,
            device_id={axis: other},
            device_id_type=MESH,
        ).start()
        return carry

    lax.fori_loop(1, size, one, 0)
    if prepare is not None:
        prepare(me)
    pltpu.make_async_copy(send_ref.at[me], place_of(me), recv_sem).start()


def layer_kernel(parts, ranks, *refs):
    (values_hbm, inner_hbm, outer_hbm, filters_ref, skip_ref, weight_hbm) = refs[:6]
    table_hbm = refs[6:16]
    out_ref = refs[16]
    (values_ref, inner_ref, outer_ref, weight_ref) = refs[17:21]
    table_refs = refs[21:31]
    (wide_ref, wide_filter_ref, data_ref, filter_ref, high_ref, low_ref, kernel_real, kernel_imag) = refs[31:39]
    (first_sends, first_recvs, second_sends, second_recvs) = (
        refs[39:41],
        refs[41:43],
        refs[43:45],
        refs[45:47],
    )
    (third_sends, third_recvs, fourth_sends) = refs[47:49], refs[49:51], refs[51:53]
    load_sems, send_sems, recv_sems = refs[53:56]
    (front_high, front_low, rear_high, rear_low, mid_high, mid_low, back_high, back_low, twist_real, twist_imag) = (
        table_refs
    )
    length, channels = values_ref.shape
    groups = filters_ref.shape[0]
    tiles = length // LANES
    rows_all = tiles * parts
    count = channels // parts
    share = count // STAGES
    chunk = min(256, rows_all)
    me = lax.axis_index("seq")
    rank = lax.axis_index("chan")

    pairs = [
        (values_hbm, values_ref),
        (inner_hbm, inner_ref),
        (outer_hbm, outer_ref),
        *zip(table_hbm, table_refs),
        (weight_hbm, weight_ref),
    ]
    loads = [
        pltpu.make_async_copy(source, target, load_sems.at[i])
        for i, (source, target) in enumerate(pairs)
    ]
    for load in loads:
        load.start()

    barrier = pltpu.get_barrier_semaphore()

    def greet(axis, place, size):
        def one(step, carry):
            other = lax.rem(place + step, size)
            pl.semaphore_signal(barrier, inc=1, device_id={axis: other}, device_id_type=MESH)
            return carry

        lax.fori_loop(1, size, one, 0)

    greet("seq", me, parts)
    greet("chan", rank, ranks)

    for tile in range(tiles):
        wide_filter_ref[pl.ds(tile, groups, stride=tiles), :] = filters_ref[
            :, pl.ds(tile * LANES, LANES)
        ].astype(F32)
    loads[0].wait()
    loads[1].wait()
    for tile in range(tiles):
        rows = pl.ds(tile * LANES, LANES)
        signal = inner_ref[rows, :].astype(F32) * values_ref[rows, :].astype(F32)
        wide_ref[pl.ds(tile, channels, stride=tiles), :] = signal.T
    own = share * tiles
    for part in range(parts):
        group = part * groups // parts
        first_sends[0][part, :tiles, :] = wide_filter_ref[pl.ds(group * tiles, tiles), :].astype(BF16)
        for stage in range(STAGES):
            offset = tiles if stage == 0 else 0
            first_sends[stage][part, pl.ds(offset, own), :] = wide_ref[
                pl.ds(part * count * tiles + stage * own, own), :
            ].astype(BF16)
    pl.semaphore_wait(barrier, parts + ranks - 2)
    for stage in range(STAGES):
        exchange(
            "seq",
            me,
            parts,
            first_sends[stage],
            lambda place, stage=stage: first_recvs[stage].at[place],
            send_sems.at[stage],
            recv_sems.at[stage],
        )
    for load in loads[3:13]:
        load.wait()

    def forward(columns, rows):
        return dot(front_high[rows, :], columns) + dot(front_low[rows, :], columns)

    def convolve(stage):
        moved_ref = first_recvs[stage]
        offset = tiles if stage == 0 else 0
        for part in range(parts):
            rows = pl.ds(part * tiles, tiles)
            for channel in range(share):
                data_ref[rows, pl.ds(channel * LANES, LANES)] = moved_ref[
                    part, pl.ds(offset + channel * tiles, tiles), :
                ]
            if stage == 0:
                filter_ref[rows, :] = moved_ref[part, :tiles, :]

        def chunk_step(step, carry):
            start = pl.multiple_of(step * chunk, chunk)
            real_rows = pl.ds(start, chunk)
            imag_rows = pl.ds(pl.multiple_of(start + rows_all, chunk), chunk)
            turn_real, turn_imag = twist_real[real_rows, :], twist_imag[real_rows, :]

            def spectrum(real, imag):
                turned = jnp.concatenate(
                    [real * turn_real - imag * turn_imag, real * turn_imag + imag * turn_real], axis=1
                )
                both = dot3(turned, mid_high[...], mid_low[...])
                return both[:, :LANES], both[:, LANES:]

            if stage == 0:
                kernel = filter_ref[...]
                kernel_real[real_rows, :], kernel_imag[real_rows, :] = spectrum(
                    forward(kernel, real_rows), forward(kernel, imag_rows)
                )
            data = data_ref[...]
            all_real, all_imag = forward(data, real_rows), forward(data, imag_rows)
            for channel in range(share):
                lanes = slice(channel * LANES, (channel + 1) * LANES)
                real, imag = spectrum(all_real[:, lanes], all_imag[:, lanes])
                product = jnp.concatenate(
                    [
                        real * kernel_real[real_rows, :] - imag * kernel_imag[real_rows, :],
                        real * kernel_imag[real_rows, :] + imag * kernel_real[real_rows, :],
                    ],
                    axis=1,
                )
                both = dot3(product, back_high[...], back_low[...])
                real, imag = both[:, :LANES], both[:, LANES:]
                high, low = halves(real * turn_real + imag * turn_imag)
                high_ref[real_rows, lanes], low_ref[real_rows, lanes] = high, low
                high, low = halves(imag * turn_real - real * turn_imag)
                high_ref[imag_rows, lanes], low_ref[imag_rows, lanes] = high, low
            return carry

        lax.fori_loop(0, rows_all // chunk, chunk_step, 0)

        def rear_step(step, carry):
            rows = pl.ds(pl.multiple_of(step * chunk, chunk), chunk)
            high, low = high_ref[...], low_ref[...]
            result = dot(rear_high[rows, :], high) + (
                dot(rear_low[rows, :], high) + dot(rear_high[rows, :], low)
            )
            result = result.astype(BF16)
            several = chunk // tiles
            for channel in range(share):
                second_sends[stage][pl.ds(step * several, several), pl.ds(channel * tiles, tiles), :] = (
                    result[:, channel * LANES : (channel + 1) * LANES].reshape(several, tiles, LANES)
                )
            return carry

        lax.fori_loop(0, rows_all // chunk, rear_step, 0)

    for stage in range(STAGES):
        wait_all(first_recvs[stage], recv_sems.at[stage])
        convolve(stage)
        exchange(
            "seq",
            me,
            parts,
            second_sends[stage],
            lambda place, stage=stage: second_recvs[stage].at[place],
            send_sems.at[STAGES + stage],
            recv_sems.at[STAGES + stage],
        )
    loads[2].wait()
    loads[13].wait()
    for stage in range(STAGES):
        wait_all(second_recvs[stage], recv_sems.at[STAGES + stage])
        for part in range(parts):
            wide_ref[pl.ds((part * count + stage * share) * tiles, own), :] = second_recvs[stage][
                part
            ].astype(F32)

    block = tiles // (ranks * STAGES)
    for stage in range(STAGES):

        def gate(other, stage=stage):
            for i in range(block):
                tile = (other * STAGES + stage) * block + i
                rows = pl.ds(pl.multiple_of(tile * LANES, LANES), LANES)
                conv = wide_ref[pl.ds(tile, channels, stride=tiles), :].T
                signal = inner_ref[rows, :].astype(F32) * values_ref[rows, :].astype(F32)
                signal = signal.astype(BF16).astype(F32)
                gated = outer_ref[rows, :].astype(F32) * (conv + skip_ref[...] * signal)
                third_sends[stage][other, pl.ds(i * LANES, LANES), :] = gated.astype(BF16)

        exchange(
            "chan",
            rank,
            ranks,
            third_sends[stage],
            lambda place, stage=stage: third_recvs[stage].at[place],
            send_sems.at[2 * STAGES + stage],
            recv_sems.at[2 * STAGES + stage],
            gate,
        )

    for stage in range(STAGES):
        wait_all(third_recvs[stage], recv_sems.at[2 * STAGES + stage])
        joined = jnp.concatenate([third_recvs[stage][other] for other in range(ranks)], axis=1)
        for other in range(0, ranks, 2):
            mixed = dot(joined, weight_ref[:, pl.ds(other * channels, 2 * channels)]).astype(BF16)
            fourth_sends[stage][other] = mixed[:, :channels]
            fourth_sends[stage][other + 1] = mixed[:, channels:]
        exchange(
            "chan",
            rank,
            ranks,
            fourth_sends[stage],
            lambda place, stage=stage: out_ref.at[place, pl.ds(stage * block * LANES, block * LANES)],
            send_sems.at[3 * STAGES + stage],
            recv_sems.at[3 * STAGES + stage],
        )
    for stage in range(STAGES):
        wait_all(
            out_ref.at[:, pl.ds(stage * block * LANES, block * LANES)], recv_sems.at[3 * STAGES + stage]
        )
    for phase, (refs_of, size) in enumerate(
        [(first_sends, parts), (second_sends, parts), (third_sends, ranks), (fourth_sends, ranks)]
    ):
        for stage in range(STAGES):
            wait_all(refs_of[stage].at[pl.ds(0, size - 1)], send_sems.at[phase * STAGES + stage])


def shards(values, inner_gate, outer_gate, filters, skip, w_out):
    parts = lax.axis_size("seq")
    ranks = lax.axis_size("chan")
    length, channels = values.shape
    groups = filters.shape[1]
    tiles = length // LANES
    rows_all = tiles * parts
    count = channels // parts
    share = count // STAGES
    own = share * tiles
    positions = length // ranks
    constants = [jnp.asarray(table) for table in tables(rows_all)]
    any_spec = pl.BlockSpec(memory_space=pl.ANY)
    vmem_spec = pl.BlockSpec(memory_space=pltpu.VMEM)
    local = pltpu.VMEM((length, channels), BF16)
    first = [pltpu.VMEM((parts, own + (tiles if s == 0 else 0), LANES), BF16) for s in range(STAGES)]
    second = [pltpu.VMEM((parts, own, LANES), BF16)] * STAGES
    third = [pltpu.VMEM((ranks, positions // STAGES, channels), BF16)] * STAGES
    mixed = pl.pallas_call(
        functools.partial(layer_kernel, parts, ranks),
        out_shape=jax.ShapeDtypeStruct((ranks, positions, channels), BF16),
        in_specs=[any_spec] * 3 + [vmem_spec] * 2 + [any_spec] * 11,
        out_specs=any_spec,
        scratch_shapes=[
            local,
            local,
            local,
            pltpu.VMEM(w_out.shape, BF16),
            *[pltpu.VMEM(table.shape, table.dtype) for table in constants],
            pltpu.VMEM((channels * tiles, LANES), F32),
            pltpu.VMEM((groups * tiles, LANES), F32),
            pltpu.VMEM((rows_all, share * LANES), BF16),
            pltpu.VMEM((rows_all, LANES), BF16),
            pltpu.VMEM((2 * rows_all, share * LANES), BF16),
            pltpu.VMEM((2 * rows_all, share * LANES), BF16),
            pltpu.VMEM((rows_all, LANES), F32),
            pltpu.VMEM((rows_all, LANES), F32),
            *first,
            *first,
            *second,
            *second,
            *third,
            *third,
            *third,
            pltpu.SemaphoreType.DMA((14,)),
            pltpu.SemaphoreType.DMA((4 * STAGES,)),
            pltpu.SemaphoreType.DMA((4 * STAGES,)),
        ],
        compiler_params=pltpu.CompilerParams(
            collective_id=0, has_side_effects=True, vmem_limit_bytes=48 << 20
        ),
    )(values, inner_gate, outer_gate, filters.T, skip[None, :], w_out, *constants)
    return mixed.reshape(length, channels)


def solution(mesh):
    in_specs = (
        P("seq", "chan"),
        P("seq", "chan"),
        P("seq", "chan"),
        P("seq", "chan"),
        P("chan"),
        P(),
    )
    out_specs = P("seq", "chan")
    return jax.shard_map(shards, mesh=mesh, in_specs=in_specs, out_specs=out_specs, check_vma=False)
```

time: 110 us -> 83.3 us (0.76)
  the two profiles are of different devices: /device:TPU:33 before, /device:TPU:64 now
where the time goes in v2:
time: 83.3 us; the launch traced here: 82.8 us
  Pallas kernels  69.5 us (83%)
  local copies, waits for them, and re-layouts  13.3 us (16%)
    pallas_call x1, Pallas kernels, shards(): pl.pallas_call(functools.partial(layer_kernel, parts, ranks), out_shape=j...  69.5 us
    unnamed x27, local copies, waits for them, and re-layouts  13.3 us

profile of v2, /device:TPU:64, one launch (start us, length us, event | category | flops | bytes accessed | tf_op | source)
XLA Modules:
  0.0 82.8 jit_solution(16971357765125079697)
XLA Ops:
  0.0 0.0 copy-start
  0.0 1.2 %copy-done = bf16[1024,512]{1,0:T(8,128)(2,1)S(1)} copy-done((bf16[1024,512]{1,0:T(8,128)(2,1)S(1)}, bf16[1024,512]{1,0:T(8,128)(2,1)}, u32[]{:S(2)}) %copy-start) | copy-done | bytes 1048600
  1.2 0.0 copy-start.1
  1.2 1.2 %copy-done.1 = bf16[1024,512]{1,0:T(8,128)(2,1)S(1)} copy-done((bf16[1024,512]{1,0:T(8,128)(2,1)S(1)}, bf16[1024,512]{1,0:T(8,128)(2,1)}, u32[]{:S(2)}) %copy-start.1) | copy-done | bytes 1048600
  2.5 0.0 copy-start.2
  2.5 1.0 %copy-done.2 = bf16[2048,128]{1,0:T(8,128)(2,1)S(1)} copy-done((bf16[2048,128]{1,0:T(8,128)(2,1)S(1)}, bf16[2048,128]{1,0:T(8,128)(2,1)}, u32[]{:S(2)}) %copy-start.2) | copy-done | bytes 524312
  3.5 0.0 copy-start.3
  3.5 1.0 %copy-done.3 = bf16[2048,128]{1,0:T(8,128)(2,1)S(1)} copy-done((bf16[2048,128]{1,0:T(8,128)(2,1)S(1)}, bf16[2048,128]{1,0:T(8,128)(2,1)}, u32[]{:S(2)}) %copy-start.3) | copy-done | bytes 524312
  4.5 0.0 copy-start.4
  4.5 1.0 %copy-done.4 = bf16[2048,128]{1,0:T(8,128)(2,1)S(1)} copy-done((bf16[2048,128]{1,0:T(8,128)(2,1)S(1)}, bf16[2048,128]{1,0:T(8,128)(2,1)}, u32[]{:S(2)}) %copy-start.4) | copy-done | bytes 524312
  5.6 0.0 copy-start.5
  5.6 0.9 %copy-done.5 = f32[512,128]{1,0:T(8,128)S(1)} copy-done((f32[512,128]{1,0:T(8,128)S(1)}, f32[512,128]{1,0:T(8,128)}, u32[]{:S(2)}) %copy-start.5) | copy-done | bytes 262168
  6.5 0.0 copy-start.6
  6.5 0.9 %copy-done.6 = f32[512,128]{1,0:T(8,128)S(1)} copy-done((f32[512,128]{1,0:T(8,128)S(1)}, f32[512,128]{1,0:T(8,128)}, u32[]{:S(2)}) %copy-start.6) | copy-done | bytes 262168
  7.5 0.0 copy-start.7
  7.5 0.9 %copy-done.7 = bf16[256,256]{1,0:T(8,128)(2,1)S(1)} copy-done((bf16[256,256]{1,0:T(8,128)(2,1)S(1)}, bf16[256,256]{1,0:T(8,128)(2,1)}, u32[]{:S(2)}) %copy-start.7) | copy-done | bytes 131096
  8.4 0.0 copy-start.8
  8.4 0.9 %copy-done.8 = bf16[256,256]{1,0:T(8,128)(2,1)S(1)} copy-done((bf16[256,256]{1,0:T(8,128)(2,1)S(1)}, bf16[256,256]{1,0:T(8,128)(2,1)}, u32[]{:S(2)}) %copy-start.8) | copy-done | bytes 131096
  9.3 0.0 copy-start.9
  9.3 0.9 %copy-done.9 = bf16[256,256]{1,0:T(8,128)(2,1)S(1)} copy-done((bf16[256,256]{1,0:T(8,128)(2,1)S(1)}, bf16[256,256]{1,0:T(8,128)(2,1)}, u32[]{:S(2)}) %copy-start.9) | copy-done | bytes 131096
  10.2 0.0 copy-start.10
  10.2 0.9 %copy-done.10 = bf16[256,256]{1,0:T(8,128)(2,1)S(1)} copy-done((bf16[256,256]{1,0:T(8,128)(2,1)S(1)}, bf16[256,256]{1,0:T(8,128)(2,1)}, u32[]{:S(2)}) %copy-start.10) | copy-done | bytes 131096
  11.1 0.0 copy-start.11
  11.1 0.8 copy-done.11
  11.9 0.0 copy-start.12
  11.9 0.7 copy-done.12
  12.5 69.5 %shard_map.154 = bf16[8,256,128]{2,1,0:T(8,128)(2,1)S(1)} custom-call(bf16[2048,128]{1,0:T(8,128)(2,1)S(1)} %copy-done.2, bf16[2048,128]{1,0:T(8,128)(2,1)S(1)} %copy-done.3, bf16[2048,128]{1,0:T(8,128)(2,1)S(1)} %copy-done.4, bf16[8,2048]{1,0:T(8,128)(2,1)S(1)} %bitcast.4, f32[1,128]{1,0:T(1,128)S(1)} %bitcast.5, bf16[1024,1024]{1,0:T(8,128)(2,1)} %refs_5_.1, ...), custom_call_target="tpu_custom_call" | custom-call | tf_op jit(solution)/shard_map/pallas_call | solution.py:337
  82.0 0.8 copy.18
Async XLA Ops:
  0.0 1.2 %copy-start = (bf16[1024,512]{1,0:T(8,128)(2,1)S(1)}, bf16[1024,512]{1,0:T(8,128)(2,1)}, u32[]{:S(2)}) copy-start(bf16[1024,512]{1,0:T(8,128)(2,1)} %constant.21.clone.refs_7_) | copy-start | bytes 3145732
  1.2 1.2 %copy-start.1 = (bf16[1024,512]{1,0:T(8,128)(2,1)S(1)}, bf16[1024,512]{1,0:T(8,128)(2,1)}, u32[]{:S(2)}) copy-start(bf16[1024,512]{1,0:T(8,128)(2,1)} %constant.20.clone.refs_6_) | copy-start | bytes 3145732
  2.5 1.0 %copy-start.2 = (bf16[2048,128]{1,0:T(8,128)(2,1)S(1)}, bf16[2048,128]{1,0:T(8,128)(2,1)}, u32[]{:S(2)}) copy-start(bf16[2048,128]{1,0:T(8,128)(2,1)} %refs_0_.1) | copy-start | bytes 1572868
  3.5 1.0 %copy-start.3 = (bf16[2048,128]{1,0:T(8,128)(2,1)S(1)}, bf16[2048,128]{1,0:T(8,128)(2,1)}, u32[]{:S(2)}) copy-start(bf16[2048,128]{1,0:T(8,128)(2,1)} %refs_1_.1) | copy-start | bytes 1572868
  4.5 1.0 %copy-start.4 = (bf16[2048,128]{1,0:T(8,128)(2,1)S(1)}, bf16[2048,128]{1,0:T(8,128)(2,1)}, u32[]{:S(2)}) copy-start(bf16[2048,128]{1,0:T(8,128)(2,1)} %refs_2_.1) | copy-start | bytes 1572868
  5.6 0.9 %copy-start.5 = (f32[512,128]{1,0:T(8,128)S(1)}, f32[512,128]{1,0:T(8,128)}, u32[]{:S(2)}) copy-start(f32[512,128]{1,0:T(8,128)} %constant.29.clone.refs_15_) | copy-start | bytes 786436
  6.5 0.9 %copy-start.6 = (f32[512,128]{1,0:T(8,128)S(1)}, f32[512,128]{1,0:T(8,128)}, u32[]{:S(2)}) copy-start(f32[512,128]{1,0:T(8,128)} %constant.28.clone.refs_14_) | copy-start | bytes 786436
  7.5 0.9 %copy-start.7 = (bf16[256,256]{1,0:T(8,128)(2,1)S(1)}, bf16[256,256]{1,0:T(8,128)(2,1)}, u32[]{:S(2)}) copy-start(bf16[256,256]{1,0:T(8,128)(2,1)} %constant.27.clone.refs_13_) | copy-start | bytes 393220
  8.4 0.9 %copy-start.8 = (bf16[256,256]{1,0:T(8,128)(2,1)S(1)}, bf16[256,256]{1,0:T(8,128)(2,1)}, u32[]{:S(2)}) copy-start(bf16[256,256]{1,0:T(8,128)(2,1)} %constant.26.clone.refs_12_) | copy-start | bytes 393220
  9.3 0.9 %copy-start.9 = (bf16[256,256]{1,0:T(8,128)(2,1)S(1)}, bf16[256,256]{1,0:T(8,128)(2,1)}, u32[]{:S(2)}) copy-start(bf16[256,256]{1,0:T(8,128)(2,1)} %constant.25.clone.refs_11_) | copy-start | bytes 393220
  10.2 0.9 %copy-start.10 = (bf16[256,256]{1,0:T(8,128)(2,1)S(1)}, bf16[256,256]{1,0:T(8,128)(2,1)}, u32[]{:S(2)}) copy-start(bf16[256,256]{1,0:T(8,128)(2,1)} %constant.24.clone.refs_10_) | copy-start | bytes 393220
  11.1 0.8 copy-start.11
  11.9 0.7 copy-start.12

commit v3 on v2

--- a/solution.py
+++ b/solution.py
@@ -99,7 +99,8 @@
         refs[45:47],
     )
     (third_sends, third_recvs, fourth_sends) = refs[47:49], refs[49:51], refs[51:53]
-    load_sems, send_sems, recv_sems = refs[53:56]
+    load_sems, send_sems, recv_sems, filter_send, filter_recv = refs[53:58]
+    filter_sends, filter_moved = refs[58:60]
     (front_high, front_low, rear_high, rear_low, mid_high, mid_low, back_high, back_low, twist_real, twist_imag) = (
         table_refs
     )
@@ -137,8 +138,8 @@
 
         lax.fori_loop(1, size, one, 0)
 
+    greet("chan", rank, ranks)
     greet("seq", me, parts)
-    greet("chan", rank, ranks)
 
     for tile in range(tiles):
         wide_filter_ref[pl.ds(tile, groups, stride=tiles), :] = filters_ref[
@@ -151,66 +152,110 @@
         signal = inner_ref[rows, :].astype(F32) * values_ref[rows, :].astype(F32)
         wide_ref[pl.ds(tile, channels, stride=tiles), :] = signal.T
     own = share * tiles
+    filter_sends[...] = wide_filter_ref[...].astype(BF16).reshape(groups, tiles, LANES)
     for part in range(parts):
-        group = part * groups // parts
-        first_sends[0][part, :tiles, :] = wide_filter_ref[pl.ds(group * tiles, tiles), :].astype(BF16)
         for stage in range(STAGES):
-            offset = tiles if stage == 0 else 0
-            first_sends[stage][part, pl.ds(offset, own), :] = wide_ref[
+            first_sends[stage][part] = wide_ref[
                 pl.ds(part * count * tiles + stage * own, own), :
             ].astype(BF16)
     pl.semaphore_wait(barrier, parts + ranks - 2)
-    for stage in range(STAGES):
+
+    sharers = parts // groups
+    each = parts // sharers
+    kind = lax.rem(me, sharers)
+
+    def send_filter(group, carry):
+        pltpu.make_async_remote_copy(
+            src_ref=filter_sends.at[group],
+            dst_ref=filter_moved.at[kind * each + me // sharers],
+            send_sem=filter_send.at[0],
+            recv_sem=filter_recv.at[0],
+            device_id={"seq": group * sharers + lax.rem(kind + 1, sharers)},
+            device_id_type=MESH,
+        ).start()
+        return carry
+
+    lax.fori_loop(0, groups, send_filter, 0)
+
+    def send_signal(stage):
         exchange(
             "seq",
             me,
             parts,
             first_sends[stage],
-            lambda place, stage=stage: first_recvs[stage].at[place],
+            lambda place: first_recvs[stage].at[place],
             send_sems.at[stage],
             recv_sems.at[stage],
         )
+
+    send_signal(0)
+    wait_all(filter_sends, filter_recv.at[0])
+    held = filter_moved.at[pl.ds(lax.rem(kind + sharers - 1, sharers) * each, each)]
+
+    def pass_filter(step, carry):
+        pltpu.make_async_remote_copy(
+            src_ref=held,
+            dst_ref=held,
+            send_sem=filter_send.at[1],
+            recv_sem=filter_recv.at[1],
+            device_id={"seq": me - kind + lax.rem(kind + step, sharers)},
+            device_id_type=MESH,
+        ).start()
+        return carry
+
+    lax.fori_loop(1, sharers, pass_filter, 0)
+    for stage in range(1, STAGES):
+        send_signal(stage)
     for load in loads[3:13]:
         load.wait()
 
     def forward(columns, rows):
         return dot(front_high[rows, :], columns) + dot(front_low[rows, :], columns)
 
+    def chunk_rows(step):
+        start = pl.multiple_of(step * chunk, chunk)
+        return pl.ds(start, chunk), pl.ds(pl.multiple_of(start + rows_all, chunk), chunk)
+
+    def spectrum(real, imag, turn_real, turn_imag):
+        turned = jnp.concatenate(
+            [real * turn_real - imag * turn_imag, real * turn_imag + imag * turn_real], axis=1
+        )
+        both = dot3(turned, mid_high[...], mid_low[...])
+        return both[:, :LANES], both[:, LANES:]
+
+    def filter_step(step, carry):
+        real_rows, imag_rows = chunk_rows(step)
+        kernel = filter_ref[...]
+        kernel_real[real_rows, :], kernel_imag[real_rows, :] = spectrum(
+            forward(kernel, real_rows),
+            forward(kernel, imag_rows),
+            twist_real[real_rows, :],
+            twist_imag[real_rows, :],
+        )
+        return carry
+
+    wait_all(filter_moved.at[pl.ds(0, parts - each)], filter_recv.at[1])
+    for part in range(parts):
+        filter_ref[pl.ds(part * tiles, tiles), :] = filter_moved[part % sharers * each + part // sharers]
+    lax.fori_loop(0, rows_all // chunk, filter_step, 0)
+
     def convolve(stage):
         moved_ref = first_recvs[stage]
-        offset = tiles if stage == 0 else 0
         for part in range(parts):
             rows = pl.ds(part * tiles, tiles)
             for channel in range(share):
                 data_ref[rows, pl.ds(channel * LANES, LANES)] = moved_ref[
-                    part, pl.ds(offset + channel * tiles, tiles), :
+                    part, pl.ds(channel * tiles, tiles), :
                 ]
-            if stage == 0:
-                filter_ref[rows, :] = moved_ref[part, :tiles, :]
 
         def chunk_step(step, carry):
-            start = pl.multiple_of(step * chunk, chunk)
-            real_rows = pl.ds(start, chunk)
-            imag_rows = pl.ds(pl.multiple_of(start + rows_all, chunk), chunk)
+            real_rows, imag_rows = chunk_rows(step)
             turn_real, turn_imag = twist_real[real_rows, :], twist_imag[real_rows, :]
-
-            def spectrum(real, imag):
-                turned = jnp.concatenate(
-                    [real * turn_real - imag * turn_imag, real * turn_imag + imag * turn_real], axis=1
-                )
-                both = dot3(turned, mid_high[...], mid_low[...])
-                return both[:, :LANES], both[:, LANES:]
-
-            if stage == 0:
-                kernel = filter_ref[...]
-                kernel_real[real_rows, :], kernel_imag[real_rows, :] = spectrum(
-                    forward(kernel, real_rows), forward(kernel, imag_rows)
-                )
             data = data_ref[...]
             all_real, all_imag = forward(data, real_rows), forward(data, imag_rows)
             for channel in range(share):
                 lanes = slice(channel * LANES, (channel + 1) * LANES)
-                real, imag = spectrum(all_real[:, lanes], all_imag[:, lanes])
+                real, imag = spectrum(all_real[:, lanes], all_imag[:, lanes], turn_real, turn_imag)
                 product = jnp.concatenate(
                     [
                         real * kernel_real[real_rows, :] - imag * kernel_imag[real_rows, :],
@@ -309,6 +354,8 @@
         wait_all(
             out_ref.at[:, pl.ds(stage * block * LANES, block * LANES)], recv_sems.at[3 * STAGES + stage]
         )
+    wait_all(filter_sends, filter_send.at[0])
+    wait_all(filter_moved.at[pl.ds(0, parts - each)], filter_send.at[1])
     for phase, (refs_of, size) in enumerate(
         [(first_sends, parts), (second_sends, parts), (third_sends, ranks), (fourth_sends, ranks)]
     ):
@@ -328,17 +375,16 @@
     own = share * tiles
     positions = length // ranks
     constants = [jnp.asarray(table) for table in tables(rows_all)]
-    any_spec = pl.BlockSpec(memory_space=pl.ANY)
+    hbm_spec = pl.BlockSpec(memory_space=pltpu.HBM)
     vmem_spec = pl.BlockSpec(memory_space=pltpu.VMEM)
     local = pltpu.VMEM((length, channels), BF16)
-    first = [pltpu.VMEM((parts, own + (tiles if s == 0 else 0), LANES), BF16) for s in range(STAGES)]
-    second = [pltpu.VMEM((parts, own, LANES), BF16)] * STAGES
+    moved = [pltpu.VMEM((parts, own, LANES), BF16)] * STAGES
     third = [pltpu.VMEM((ranks, positions // STAGES, channels), BF16)] * STAGES
     mixed = pl.pallas_call(
         functools.partial(layer_kernel, parts, ranks),
         out_shape=jax.ShapeDtypeStruct((ranks, positions, channels), BF16),
-        in_specs=[any_spec] * 3 + [vmem_spec] * 2 + [any_spec] * 11,
-        out_specs=any_spec,
+        in_specs=[hbm_spec] * 3 + [vmem_spec] * 2 + [hbm_spec] * 11,
+        out_specs=hbm_spec,
         scratch_shapes=[
             local,
             local,
@@ -353,19 +399,20 @@
             pltpu.VMEM((2 * rows_all, share * LANES), BF16),
             pltpu.VMEM((rows_all, LANES), F32),
             pltpu.VMEM((rows_all, LANES), F32),
-            *first,
-            *first,
-            *second,
-            *second,
+            *moved * 4,
             *third,
             *third,
             *third,
             pltpu.SemaphoreType.DMA((14,)),
             pltpu.SemaphoreType.DMA((4 * STAGES,)),
             pltpu.SemaphoreType.DMA((4 * STAGES,)),
+            pltpu.SemaphoreType.DMA((2,)),
+            pltpu.SemaphoreType.DMA((2,)),
+            pltpu.VMEM((groups, tiles, LANES), BF16),
+            pltpu.VMEM((parts, tiles, LANES), BF16),
         ],
         compiler_params=pltpu.CompilerParams(
-            collective_id=0, has_side_effects=True, vmem_limit_bytes=48 << 20
+            collective_id=0, has_side_effects=True, vmem_limit_bytes=56 << 20
         ),
     )(values, inner_gate, outer_gate, filters.T, skip[None, :], w_out, *constants)
     return mixed.reshape(length, channels)

time: 83.3 us -> 66.6 us (0.80)
  local copies, waits for them, and re-layouts: 13.3 us -> 1.87 us
  Pallas kernels: 69.5 us -> 63.8 us
    unnamed x27 -> x1, local copies, waits for them, and re-layouts: 13.3 us -> 1.87 us
    pallas_call x1, Pallas kernels: 69.5 us -> 63.8 us  [shards(): pl.pallas_call(functools.partial(layer_kernel, parts, ranks), out_shape=j...]
where the time goes in v3:
time: 66.6 us; the launch traced here: 65.7 us
  Pallas kernels  63.8 us (96%)
  local copies, waits for them, and re-layouts  1.87 us (3%)
    pallas_call x1, Pallas kernels, shards(): pl.pallas_call(functools.partial(layer_kernel, parts, ranks), out_shape=j...  63.8 us
    unnamed x1, local copies, waits for them, and re-layouts  1.87 us

profile of v3, /device:TPU:64, one launch (start us, length us, event | category | flops | bytes accessed | tf_op | source)
XLA Modules:
  0.0 65.7 jit_solution(2150086815155721568)
XLA Ops:
  0.0 63.8 %shard_map.154 = bf16[8,256,128]{2,1,0:T(8,128)(2,1)} custom-call(bf16[2048,128]{1,0:T(8,128)(2,1)} %refs_0_.1, bf16[2048,128]{1,0:T(8,128)(2,1)} %refs_1_.1, bf16[2048,128]{1,0:T(8,128)(2,1)} %refs_2_.1, bf16[8,2048]{1,0:T(8,128)(2,1)} %bitcast.4, f32[1,128]{1,0:T(1,128)} %bitcast.5, bf16[1024,1024]{1,0:T(8,128)(2,1)} %refs_5_.1, ...), custom_call_target="tpu_custom_call" | custom-call | tf_op jit(solution)/shard_map/pallas_call | solution.py:383
  63.8 1.9 %copy.18 = bf16[2048,128]{1,0:T(8,128)(2,1)} copy(bf16[2048,128]{1,0:T(8,128)(2,1)} %bitcast.3) | data formatting | bytes 1048576

commit v4 on v3

--- a/solution.py
+++ b/solution.py
@@ -36,11 +36,15 @@
     cos, sin = np.cos(angle), np.sin(angle)
     mid = np.block([[cos, -sin], [sin, cos]])
     back = np.block([[cos, sin], [-sin, cos]])
+    front_high, front_low = split_table(front)
+    rear_high, rear_low = split_table(front.T / n)
+    mid_high, mid_low = split_table(mid)
+    back_high, back_low = split_table(back)
     return (
-        *split_table(front),
-        *split_table(front.T / n),
-        *split_table(mid),
-        *split_table(back),
+        np.concatenate([front_high, front_low], axis=1),
+        np.concatenate([rear_high, rear_high, rear_low], axis=1),
+        np.concatenate([mid_high, mid_high, mid_low], axis=0),
+        np.concatenate([back_high, back_high, back_low], axis=0),
         twist_real,
         twist_imag,
     )
@@ -55,9 +59,9 @@
     return jnp.dot(left, right, preferred_element_type=F32)
 
 
-def dot3(left, right_high, right_low):
-    left_high, left_low = halves(left)
-    return dot(left_high, right_high) + (dot(left_high, right_low) + dot(left_low, right_high))
+def dot3(left, table):
+    high, low = halves(left)
+    return dot(jnp.concatenate([high, low, high], axis=1), table)
 
 
 def wait_all(ref, sem):
@@ -87,30 +91,28 @@
 
 def layer_kernel(parts, ranks, *refs):
     (values_hbm, inner_hbm, outer_hbm, filters_ref, skip_ref, weight_hbm) = refs[:6]
-    table_hbm = refs[6:16]
-    out_ref = refs[16]
-    (values_ref, inner_ref, outer_ref, weight_ref) = refs[17:21]
-    table_refs = refs[21:31]
-    (wide_ref, wide_filter_ref, data_ref, filter_ref, high_ref, low_ref, kernel_real, kernel_imag) = refs[31:39]
+    table_hbm = refs[6:12]
+    out_ref = refs[12]
+    (values_ref, inner_ref, outer_ref, weight_ref) = refs[13:17]
+    table_refs = refs[17:23]
+    (wide_ref, wide_filter_ref, data_ref, filter_ref, split_ref, kernel_real, kernel_imag) = refs[23:30]
     (first_sends, first_recvs, second_sends, second_recvs) = (
-        refs[39:41],
-        refs[41:43],
-        refs[43:45],
-        refs[45:47],
+        refs[30:32],
+        refs[32:34],
+        refs[34:36],
+        refs[36:38],
     )
-    (third_sends, third_recvs, fourth_sends) = refs[47:49], refs[49:51], refs[51:53]
-    load_sems, send_sems, recv_sems, filter_send, filter_recv = refs[53:58]
-    filter_sends, filter_moved = refs[58:60]
-    (front_high, front_low, rear_high, rear_low, mid_high, mid_low, back_high, back_low, twist_real, twist_imag) = (
-        table_refs
-    )
+    (third_sends, third_recvs, fourth_sends) = refs[38:40], refs[40:42], refs[42:44]
+    load_sems, send_sems, recv_sems, filter_send, filter_recv = refs[44:49]
+    filter_sends, filter_moved = refs[49:51]
+    front_table, rear_table, mid_table, back_table, twist_real, twist_imag = table_refs
     length, channels = values_ref.shape
     groups = filters_ref.shape[0]
     tiles = length // LANES
     rows_all = tiles * parts
     count = channels // parts
     share = count // STAGES
-    chunk = min(256, rows_all)
+    chunk = min(512, rows_all)
     me = lax.axis_index("seq")
     rank = lax.axis_index("chan")
 
@@ -206,11 +208,11 @@
     lax.fori_loop(1, sharers, pass_filter, 0)
     for stage in range(1, STAGES):
         send_signal(stage)
-    for load in loads[3:13]:
+    for load in loads[3:9]:
         load.wait()
 
     def forward(columns, rows):
-        return dot(front_high[rows, :], columns) + dot(front_low[rows, :], columns)
+        return dot(front_table[rows, :], columns)
 
     def chunk_rows(step):
         start = pl.multiple_of(step * chunk, chunk)
@@ -220,7 +222,7 @@
         turned = jnp.concatenate(
             [real * turn_real - imag * turn_imag, real * turn_imag + imag * turn_real], axis=1
         )
-        both = dot3(turned, mid_high[...], mid_low[...])
+        both = dot3(turned, mid_table[...])
         return both[:, :LANES], both[:, LANES:]
 
     def filter_step(step, carry):
@@ -236,7 +238,9 @@
 
     wait_all(filter_moved.at[pl.ds(0, parts - each)], filter_recv.at[1])
     for part in range(parts):
-        filter_ref[pl.ds(part * tiles, tiles), :] = filter_moved[part % sharers * each + part // sharers]
+        block_of = filter_moved[part % sharers * each + part // sharers]
+        filter_ref[pl.ds(part * tiles, tiles), :] = block_of
+        filter_ref[pl.ds(rows_all + part * tiles, tiles), :] = block_of
     lax.fori_loop(0, rows_all // chunk, filter_step, 0)
 
     def convolve(stage):
@@ -244,9 +248,10 @@
         for part in range(parts):
             rows = pl.ds(part * tiles, tiles)
             for channel in range(share):
-                data_ref[rows, pl.ds(channel * LANES, LANES)] = moved_ref[
-                    part, pl.ds(channel * tiles, tiles), :
-                ]
+                lanes = pl.ds(channel * LANES, LANES)
+                block_of = moved_ref[part, pl.ds(channel * tiles, tiles), :]
+                data_ref[rows, lanes] = block_of
+                data_ref[pl.ds(rows_all + part * tiles, tiles), lanes] = block_of
 
         def chunk_step(step, carry):
             real_rows, imag_rows = chunk_rows(step)
@@ -263,23 +268,23 @@
                     ],
                     axis=1,
                 )
-                both = dot3(product, back_high[...], back_low[...])
+                both = dot3(product, back_table[...])
                 real, imag = both[:, :LANES], both[:, LANES:]
-                high, low = halves(real * turn_real + imag * turn_imag)
-                high_ref[real_rows, lanes], low_ref[real_rows, lanes] = high, low
-                high, low = halves(imag * turn_real - real * turn_imag)
-                high_ref[imag_rows, lanes], low_ref[imag_rows, lanes] = high, low
+                for rows, value in (
+                    (real_rows, real * turn_real + imag * turn_imag),
+                    (imag_rows, imag * turn_real - real * turn_imag),
+                ):
+                    high, low = halves(value)
+                    split_ref[rows, lanes] = high
+                    split_ref[pl.ds(rows.start + 2 * rows_all, chunk), lanes] = low
+                    split_ref[pl.ds(rows.start + 4 * rows_all, chunk), lanes] = high
             return carry
 
         lax.fori_loop(0, rows_all // chunk, chunk_step, 0)
 
         def rear_step(step, carry):
             rows = pl.ds(pl.multiple_of(step * chunk, chunk), chunk)
-            high, low = high_ref[...], low_ref[...]
-            result = dot(rear_high[rows, :], high) + (
-                dot(rear_low[rows, :], high) + dot(rear_high[rows, :], low)
-            )
-            result = result.astype(BF16)
+            result = dot(rear_table[rows, :], split_ref[...]).astype(BF16)
             several = chunk // tiles
             for channel in range(share):
                 second_sends[stage][pl.ds(step * several, several), pl.ds(channel * tiles, tiles), :] = (
@@ -302,7 +307,7 @@
             recv_sems.at[STAGES + stage],
         )
     loads[2].wait()
-    loads[13].wait()
+    loads[9].wait()
     for stage in range(STAGES):
         wait_all(second_recvs[stage], recv_sems.at[STAGES + stage])
         for part in range(parts):
@@ -383,7 +388,7 @@
     mixed = pl.pallas_call(
         functools.partial(layer_kernel, parts, ranks),
         out_shape=jax.ShapeDtypeStruct((ranks, positions, channels), BF16),
-        in_specs=[hbm_spec] * 3 + [vmem_spec] * 2 + [hbm_spec] * 11,
+        in_specs=[hbm_spec] * 3 + [vmem_spec] * 2 + [hbm_spec] * 7,
         out_specs=hbm_spec,
         scratch_shapes=[
             local,
@@ -393,17 +398,16 @@
             *[pltpu.VMEM(table.shape, table.dtype) for table in constants],
             pltpu.VMEM((channels * tiles, LANES), F32),
             pltpu.VMEM((groups * tiles, LANES), F32),
-            pltpu.VMEM((rows_all, share * LANES), BF16),
-            pltpu.VMEM((rows_all, LANES), BF16),
             pltpu.VMEM((2 * rows_all, share * LANES), BF16),
-            pltpu.VMEM((2 * rows_all, share * LANES), BF16),
+            pltpu.VMEM((2 * rows_all, LANES), BF16),
+            pltpu.VMEM((6 * rows_all, share * LANES), BF16),
             pltpu.VMEM((rows_all, LANES), F32),
             pltpu.VMEM((rows_all, LANES), F32),
             *moved * 4,
             *third,
             *third,
             *third,
-            pltpu.SemaphoreType.DMA((14,)),
+            pltpu.SemaphoreType.DMA((10,)),
             pltpu.SemaphoreType.DMA((4 * STAGES,)),
             pltpu.SemaphoreType.DMA((4 * STAGES,)),
             pltpu.SemaphoreType.DMA((2,)),

time: 66.6 us -> 66.1 us (level)
  no operation moved by 1% of the time
where the time goes in v4:
time: 66.1 us; the launch traced here: 65.3 us
  Pallas kernels  63.4 us (96%)
  local copies, waits for them, and re-layouts  1.87 us (3%)
    pallas_call x1, Pallas kernels, shards(): pl.pallas_call(functools.partial(layer_kernel, parts, ranks), out_shape=j...  63.4 us
    unnamed x1, local copies, waits for them, and re-layouts  1.87 us

profile of v4, /device:TPU:64, one launch (start us, length us, event | category | flops | bytes accessed | tf_op | source)
XLA Modules:
  0.0 65.3 jit_solution(12264599430640856217)
XLA Ops:
  0.0 63.4 %shard_map.118 = bf16[8,256,128]{2,1,0:T(8,128)(2,1)} custom-call(bf16[2048,128]{1,0:T(8,128)(2,1)} %refs_0_.1, bf16[2048,128]{1,0:T(8,128)(2,1)} %refs_1_.1, bf16[2048,128]{1,0:T(8,128)(2,1)} %refs_2_.1, bf16[8,2048]{1,0:T(8,128)(2,1)} %bitcast.4, f32[1,128]{1,0:T(1,128)} %bitcast.5, bf16[1024,1024]{1,0:T(8,128)(2,1)} %refs_5_.1, ...), custom_call_target="tpu_custom_call" | custom-call | tf_op jit(solution)/shard_map/pallas_call | solution.py:388
  63.4 1.9 %copy.14 = bf16[2048,128]{1,0:T(8,128)(2,1)} copy(bf16[2048,128]{1,0:T(8,128)(2,1)} %bitcast.3) | data formatting | bytes 1048576
